TPU v7x, 32 devices: a whole 2x2x4 slice. The times are simulated.
32 devices in a mesh: dp: 4 (over x, core), seq: 4 (over z), tensor: 2 (over y).
Axes of the slice: x: 2, y: 2, z: 4, core: 2. Of those that a mesh axis runs over, the one named last changes fastest.
Arguments:
- queries: bfloat16 [4, 2048, 1024], P('dp', 'seq', 'tensor'), may hold values from -6 to 6
- key_vectors: bfloat16 [4, 2048, 1024], P('dp', 'seq', 'tensor'), may hold values from -6 to 6
- value_vectors: bfloat16 [4, 2048, 1024], P('dp', 'seq', 'tensor'), may hold values from -6 to 6
- log_decay: float32 [4, 8, 2048], P('dp', 'tensor'), may hold values from -0.75 to 0
- w_out: bfloat16 [1024, 3072], P('tensor'), may hold values from -0.1875 to 0.1875
- grad_out: bfloat16 [4, 2048, 3072], P('dp', 'seq', 'tensor'), may hold values from -6 to 6
Outputs:
- grad_queries: bfloat16 [4, 2048, 1024], P('dp', 'seq', 'tensor')
- grad_keys: bfloat16 [4, 2048, 1024], P('dp', 'seq', 'tensor')
- grad_values: bfloat16 [4, 2048, 1024], P('dp', 'seq', 'tensor')
- grad_w_t: float32 [3072, 1024], P(('dp', 'seq'), 'tensor')
All inputs are finite; a program needn't handle non-finite values.
Results may differ from a plain program's by a relative error of at most 0.015.
Values may be sent and summed in bfloat16 or wider, within the bound.
No kernel may reach another device: no remote copies, remote signals or barrier semaphores. Data moves between devices by JAX's collectives and lax.ppermute only.
A program may use at most 64 MiB of HBM per device.

v0:
```python
import math
import jax
import jax.numpy as jnp
from jax import lax
from jax.sharding import PartitionSpec as P

D = 3072
highest_precision = lax.Precision.HIGHEST


def decay_matrix(cumulative):
    size_now = cumulative.shape[-1]
    later_pos = lax.broadcasted_iota(jnp.int32, (size_now, size_now), 0)
    earlier_pos = lax.broadcasted_iota(jnp.int32, (size_now, size_now), 1)
    lower = later_pos >= earlier_pos
    spread = cumulative[..., :, None] - cumulative[..., None, :]
    return jnp.where(lower, jnp.exp(jnp.where(lower, spread, 0.0)), 0.0)


def local(queries, key_vectors, value_vectors, log_decay, w_out, grad_out):
    micro_count, row_count, feature_width = queries.shape
    head_count = log_decay.shape[1]
    head_dim = feature_width // head_count
    flat_size = head_dim * head_dim
    seq_count = lax.axis_size("seq")
    seq_index = lax.axis_index("seq")
    inverse = 1.0 / head_dim
    grad_scale = 1.0 / math.sqrt(micro_count * lax.axis_size("dp") * row_count * seq_count)
    block_totals = jnp.sum(log_decay.reshape(micro_count, head_count, seq_count, row_count), axis=3)
    block_ends = jnp.cumsum(block_totals, axis=2)
    block_starts = block_ends - block_totals
    start_here = lax.dynamic_index_in_dim(block_starts, seq_index, axis=2, keepdims=False)
    end_here = lax.dynamic_index_in_dim(block_ends, seq_index, axis=2, keepdims=False)
    local_decay = lax.dynamic_slice_in_dim(log_decay, seq_index * row_count, row_count, axis=2)
    cumulative = jnp.cumsum(local_decay, axis=2)
    own_total = cumulative[:, :, -1]
    decay_mask = decay_matrix(cumulative)
    from_start = jnp.transpose(jnp.exp(cumulative), (0, 2, 1))[..., None]
    to_end = jnp.transpose(jnp.exp(own_total[:, :, None] - cumulative), (0, 2, 1))[..., None]
    query_heads = queries.reshape(micro_count, row_count, head_count, head_dim)
    key_heads = key_vectors.reshape(micro_count, row_count, head_count, head_dim)
    value_heads = value_vectors.reshape(micro_count, row_count, head_count, head_dim)
    query_float = query_heads.astype(jnp.float32)
    key_float = key_heads.astype(jnp.float32)
    value_float = value_heads.astype(jnp.float32)
    empty_states = jnp.zeros((micro_count, head_count, flat_size), jnp.float32)
    scores = jnp.einsum(
        "mthd,mshd->mhts", query_heads, key_heads, preferred_element_type=jnp.float32
    )
    weights = (scores * decay_mask * inverse).astype(jnp.bfloat16)
    local_state = jnp.einsum(
        "mshd,mshe->mhde", key_float * to_end, value_float, precision=highest_precision
    )
    shard_piece = lax.all_gather(
        local_state.reshape(1, micro_count, head_count, flat_size).astype(jnp.bfloat16),
        "seq",
        axis=0,
        tiled=True,
    ).astype(jnp.float32)
    piece_rows = shard_piece.shape[0]
    position = jnp.arange(piece_rows, dtype=jnp.int32)
    factor = jnp.where(
        position[None, None, :] < seq_index,
        jnp.exp(jnp.minimum(start_here[:, :, None] - block_ends, 0.0)),
        0.0,
    )
    incoming = empty_states + jnp.einsum(
        "nmhx,mhn->mhx", shard_piece, factor, precision=highest_precision
    )
    carried = incoming.reshape(micro_count, head_count, head_dim, head_dim)
    within_block = jnp.einsum(
        "mhts,mshd->mthd", weights, value_heads, preferred_element_type=jnp.float32
    )
    from_carried = jnp.einsum(
        "mthd,mhde->mthe", query_float * from_start, carried, precision=highest_precision
    )
    attn_out = (
        (within_block + from_carried * inverse)
        .astype(jnp.bfloat16)
        .reshape(micro_count, row_count, feature_width)
    )
    shard_piece = lax.all_gather(grad_out, "tensor", axis=2, tiled=True)
    attn_running = jnp.einsum("mcd,fd->mcf", shard_piece, w_out, preferred_element_type=jnp.float32)
    column_block = jnp.einsum(
        "mcd,mcf->df", shard_piece, attn_out, preferred_element_type=jnp.float32
    )
    grad_attn = attn_running.astype(jnp.bfloat16)
    rounded = lax.optimization_barrier((column_block * grad_scale).astype(jnp.bfloat16)).astype(
        jnp.float32
    )
    reordered = jnp.transpose(
        rounded.reshape(
            lax.axis_size("dp"), seq_count, D // (lax.axis_size("dp") * seq_count), feature_width
        ),
        (1, 0, 2, 3),
    ).reshape(D, feature_width)
    reduced = lax.psum_scatter(
        reordered.astype(jnp.bfloat16), "seq", scatter_dimension=0, tiled=True
    )
    grad_w_t = lax.psum_scatter(reduced, "dp", scatter_dimension=0, tiled=True).astype(jnp.float32)
    grad_heads = grad_attn.reshape(micro_count, row_count, head_count, head_dim)
    grad_float = grad_heads.astype(jnp.float32)
    grad_scores = jnp.einsum(
        "mthd,mshd->mhts", grad_heads, value_heads, preferred_element_type=jnp.float32
    )
    grad_weights = (grad_scores * decay_mask * inverse).astype(jnp.bfloat16)
    local_back = (
        jnp.einsum(
            "mthd,mthe->mhde", query_float * from_start, grad_float, precision=highest_precision
        )
        * inverse
    )
    shard_piece = lax.all_gather(
        local_back.reshape(1, micro_count, head_count, flat_size).astype(jnp.bfloat16),
        "seq",
        axis=0,
        tiled=True,
    ).astype(jnp.float32)
    piece_rows = shard_piece.shape[0]
    position = jnp.arange(piece_rows, dtype=jnp.int32)
    factor = jnp.where(
        position[None, None, :] > seq_index,
        jnp.exp(jnp.minimum(block_starts - end_here[:, :, None], 0.0)),
        0.0,
    )
    outgoing = empty_states + jnp.einsum(
        "nmhx,mhn->mhx", shard_piece, factor, precision=highest_precision
    )
    back_state = outgoing.reshape(micro_count, head_count, head_dim, head_dim)
    grad_queries = (
        jnp.einsum("mhts,mshd->mthd", grad_weights, key_heads, preferred_element_type=jnp.float32)
        + jnp.einsum(
            "mthe,mhde->mthd", grad_float * from_start, carried, precision=highest_precision
        )
        * inverse
    )
    grad_keys = jnp.einsum(
        "mhts,mthd->mshd", grad_weights, query_heads, preferred_element_type=jnp.float32
    ) + jnp.einsum("mshe,mhde->mshd", value_float * to_end, back_state, precision=highest_precision)
    grad_values = jnp.einsum(
        "mhts,mthd->mshd", weights, grad_heads, preferred_element_type=jnp.float32
    ) + jnp.einsum("mshd,mhde->mshe", key_float * to_end, back_state, precision=highest_precision)
    out_shape = (micro_count, row_count, feature_width)
    return (
        grad_queries.astype(jnp.bfloat16).reshape(out_shape),
        grad_keys.astype(jnp.bfloat16).reshape(out_shape),
        grad_values.astype(jnp.bfloat16).reshape(out_shape),
        grad_w_t,
    )


def solution(mesh):
    in_specs = (
        P("dp", "seq", "tensor"),
        P("dp", "seq", "tensor"),
        P("dp", "seq", "tensor"),
        P("dp", "tensor", None),
        P("tensor", None),
        P("dp", "seq", "tensor"),
    )
    out_specs = (
        P("dp", "seq", "tensor"),
        P("dp", "seq", "tensor"),
        P("dp", "seq", "tensor"),
        P(("dp", "seq"), "tensor"),
    )
    return jax.shard_map(local, mesh=mesh, in_specs=in_specs, out_specs=out_specs, check_vma=False)
```

profile of v0, /device:TPU:0, one launch (start us, length us, event | category | flops | bytes accessed | tf_op | source)
XLA Modules:
  0.0 169.6 jit_solution(3306231275859728322)
XLA Ops:
  7.2 0.7 all-gather.2.cloned.1.call-update
  8.0 0.8 constant_dynamic-slice_fusion
  8.8 1.2 reduce-window.6
  10.2 0.2 reduce-window.9
  10.4 0.9 copy.129
  11.2 0.8 reshape.429
  12.3 2.0 %reshape.419 = bf16[512,4,128]{2,1,0:T(4,128)(2,1)} reshape(bf16[1,512,512]{2,1,0:T(8,128)(2,1)} %param.8) | data formatting | bytes 1048576 | tf_op jit(solution)/shard_map/reshape.6
  14.2 2.0 %reshape.425 = bf16[512,4,128]{2,1,0:T(4,128)(2,1)} reshape(bf16[1,512,512]{2,1,0:T(8,128)(2,1)} %param.7) | data formatting | bytes 1048576 | tf_op jit(solution)/shard_map/reshape.13
  16.2 1.7 exponential_bitcast_fusion
  17.9 1.1 copy.100
  19.1 0.2 reduce_window_sum.55
  19.3 0.8 exponential_bitcast_fusion.1
  20.0 1.1 copy.96
  21.1 2.6 %convolution_convert_fusion = bf16[4,128,128]{2,1,0:T(8,128)(2,1)S(1)} fusion(f32[512,4]{0,1:T(4,128)S(1)} %copy.96, bf16[512,4,128]{2,1,0:T(4,128)(2,1)} %reshape.425, bf16[512,4,128]{2,1,0:T(4,128)(2,1)} %reshape.419), kind=kOutput, calls=%fused_computation.24 | convolution fusion | flops 403243008 | bytes 1187840 | tf_op jit(solution)/shard_map/mshd,mshe->mhde/dot_general | solution.py:51
  23.8 0.2 dynamic-slice_reduce_fusion
  24.0 17.4 %all_gather.10 = bf16[4,1,4,16384]{3,2,1,0:T(4,128)(2,1)S(1)} all-gather(bf16[1,1,4,16384]{3,2,1,0:T(4,128)(2,1)S(1)} %convert_element_type.128), channel_id=1, replica_groups=mesh['dp'=4,'seq'=4,'tensor'=2] {'seq'}, dimensions={0}, use_global_device_ids=true | all-gather | bytes 655360 | tf_op jit(solution)/shard_map/all_gather | solution.py:54
  41.5 1.3 fusion.26
  42.9 0.2 copy.191
  43.0 2.0 %reshape.432 = bf16[512,4,128]{2,1,0:T(4,128)(2,1)} reshape(bf16[1,512,512]{2,1,0:T(8,128)(2,1)} %param.6) | data formatting | bytes 1048576 | tf_op jit(solution)/shard_map/reshape.51
  45.1 2.8 %multiply_convert_fusion.1 = bf16[4,512,512]{2,1,0:T(8,128)(2,1)S(1)} fusion(f32[4,512]{1,0:T(4,128)S(1)} %bitcast_add_fusion.1, pred[512,512]{1,0:T(8,128)(4,1)S(1)} %iota_compare_fusion, bf16[512,4,128]{2,1,0:T(4,128)(2,1)} %reshape.432, bf16[512,4,128]{2,1,0:T(4,128)(2,1)} %reshape.425), kind=kOutput, calls=%fused_computation.1 | convolution fusion | flops 274726912 | bytes 3416064 | tf_op jit(solution)/shard_map/mthd,mshd->mhts/dot_general | solution.py:47
  47.9 1.3 copy-done.1
  49.2 0.8 convolution_bitcast_fusion.1
  50.1 0.2 copy-done.8
  50.3 2.2 %fusion.12 = bf16[4,128,512]{2,1,0:T(8,128)(2,1)} fusion(f32[4,128,512]{2,1,0:T(8,128)S(1)} %convolution_bitcast_fusion.1, f32[512,4]{0,1:T(4,128)S(1)} %copy.100, bf16[512,4,128]{2,1,0:T(4,128)(2,1)S(1)} %copy-done.8, f32[1,4,128,128]{3,1,2,0:T(4,128)S(1)} %bitcast.122), kind=kOutput, calls=%fused_computation.21 | convolution fusion | flops 403963904 | bytes 2367488 | tf_op jit(solution)/shard_map/mthd,mhde->mthe/dot_general | solution.py:74
  52.5 4.7 %all-gather.2.cloned.1.call-done = bf16[1,512,3072]{2,1,0:T(8,128)(2,1)} async-done(((bf16[1,512,1536]{2,1,0:T(8,128)(2,1)}), bf16[1,512,3072]{2,1,0:T(8,128)(2,1)}) %all-gather.2.cloned.1.call-update) | async-done | bytes 3145744 | tf_op jit(solution)/shard_map/all_gather | solution.py:82
  57.2 5.6 %fusion = bf16[3072,512]{0,1:T(8,128)(2,1)} fusion(bf16[512,512]{0,1:T(8,128)(2,1)} %bitcast.136, bf16[1,512,3072]{2,1,0:T(8,128)(2,1)} %all-gather.2.cloned.1.call-done), kind=kOutput, calls=%fused_computation.4 | convolution fusion | flops 1613758464 | bytes 6815744 | tf_op jit(solution)/shard_map/mcd,mcf->df/dot_general | solution.py:84
  62.8 4.7 %copy.111 = bf16[3072,512]{1,0:T(8,128)(2,1)} copy(bf16[3072,512]{0,1:T(8,128)(2,1)} %fusion) | data formatting | bytes 6291456 | tf_op jit(solution)/shard_map/optimization_barrier | solution.py:88
  67.6 3.9 %copy.112 = bf16[4,4,192,512]{3,2,1,0:T(8,128)(2,1)} copy(bf16[4,4,192,512]{3,2,0,1:T(8,128)(2,1)} %bitcast.121) | data formatting | bytes 6291456 | tf_op jit(solution)/shard_map/convert_element_type | solution.py:98
  71.4 0.2 reduce-scatter.5.cloned.1.call-start
  71.7 4.5 %fusion.6 = bf16[512,512]{0,1:T(8,128)(2,1)} fusion(bf16[512,3072]{1,0:T(8,128)(2,1)S(1)} %copy-done, bf16[1,512,3072]{2,1,0:T(8,128)(2,1)} %all-gather.2.cloned.1.call-done), kind=kOutput, calls=%fused_computation.17 | convolution fusion | flops 1610874880 | bytes 6815744 | tf_op jit(solution)/shard_map/mcd,fd->mcf/dot_general | solution.py:83
  76.2 2.0 %copy.99 = bf16[512,4,128]{2,0,1:T(8,128)(2,1)} copy(bf16[512,4,128]{0,2,1:T(8,128)(2,1)} %bitcast.126) | data formatting | bytes 1048576 | tf_op jit(solution)/shard_map/reshape.5
  78.2 3.0 %multiply_convert_fusion.2 = bf16[4,512,512]{2,1,0:T(8,128)(2,1)S(1)} fusion(bf16[512,4,128]{0,2,1:T(8,128)(2,1)} %bitcast.127, f32[4,512]{1,0:T(4,128)S(1)} %bitcast_add_fusion.1, pred[512,512]{1,0:T(8,128)(4,1)} %copy-done.10, bf16[512,4,128]{2,1,0:T(4,128)(2,1)} %reshape.419), kind=kOutput, calls=%fused_computation.2 | convolution fusion | flops 274726912 | bytes 3416064 | tf_op jit(solution)/shard_map/mthd,mshd->mhts/dot_general | solution.py:103
  81.3 1.3 copy-done.2
  82.6 0.8 convolution_bitcast_fusion.2
  83.4 0.2 copy-done.9
  83.6 2.1 %fusion.9 = bf16[4,128,512]{2,1,0:T(8,128)(2,1)} fusion(f32[4,128,512]{2,1,0:T(8,128)S(1)} %convolution_bitcast_fusion.2, bf16[512,4,128]{2,0,1:T(8,128)(2,1)S(1)} %copy-done.9, f32[512,4]{0,1:T(4,128)S(1)} %copy.100, f32[1,4,128,128]{3,1,2,0:T(4,128)S(1)} %bitcast.123), kind=kOutput, calls=%fused_computation.18 | convolution fusion | flops 403963904 | bytes 2367488 | tf_op jit(solution)/shard_map/mthe,mhde->mthd/dot_general | solution.py:132
  85.7 2.0 %copy.113 = bf16[1,512,512]{2,1,0:T(8,128)(2,1)} copy(bf16[1,512,512]{1,2,0:T(8,128)(2,1)} %bitcast.131) | data formatting | bytes 1048576
  87.8 2.5 %fusion.13 = bf16[4,128,128]{2,1,0:T(8,128)(2,1)S(1)} fusion(bf16[512,4,128]{0,2,1:T(8,128)(2,1)} %bitcast.128, f32[512,4]{0,1:T(4,128)S(1)} %copy.100, bf16[512,4,128]{2,1,0:T(4,128)(2,1)} %reshape.432), kind=kOutput, calls=%fused_computation.23 | convolution fusion | flops 403308544 | bytes 1187840 | tf_op jit(solution)/shard_map/mthd,mthe->mhde/dot_general | solution.py:108
  90.4 41.6 %reduce-scatter.3.cloned.1.call-done = bf16[768,512]{1,0:T(8,128)(2,1)} async-done(((bf16[3072,512]{1,0:T(8,128)(2,1)}), bf16[768,512]{1,0:T(8,128)(2,1)}) %reduce-scatter.3.cloned.1.call-update) | async-done | bytes 786448 | tf_op jit(solution)/shard_map/reduce_scatter | solution.py:97
  132.0 15.6 %all_gather.11 = bf16[4,1,4,16384]{3,2,1,0:T(4,128)(2,1)S(1)} all-gather(bf16[1,1,4,16384]{3,2,1,0:T(4,128)(2,1)S(1)} %convert_element_type.135), channel_id=1, replica_groups=mesh['dp'=4,'seq'=4,'tensor'=2] {'seq'}, dimensions={0}, use_global_device_ids=true | all-gather | bytes 655360 | tf_op jit(solution)/shard_map/all_gather | solution.py:113
  147.6 1.3 fusion.24
  149.2 1.5 convolution_bitcast_fusion
  150.7 2.1 %fusion.10 = bf16[4,128,512]{2,1,0:T(8,128)(2,1)} fusion(f32[4,128,512]{2,1,0:T(8,128)S(1)} %convolution_bitcast_fusion, f32[512,4]{0,1:T(4,128)S(1)} %copy.96, bf16[512,4,128]{2,1,0:T(4,128)(2,1)S(1)} %copy-done.7, f32[1,4,128,128]{3,1,2,0:T(4,128)S(1)} %bitcast.124), kind=kOutput, calls=%fused_computation.19 | convolution fusion | flops 403701760 | bytes 2367488 | tf_op jit(solution)/shard_map/mshe,mhde->mshd/dot_general | solution.py:139
  152.8 2.0 %copy.114 = bf16[1,512,512]{2,1,0:T(8,128)(2,1)} copy(bf16[1,512,512]{1,2,0:T(8,128)(2,1)} %bitcast.132) | data formatting | bytes 1048576
  154.8 2.3 %fusion.55 = f32[4,128,512]{2,1,0:T(8,128)S(1)} fusion(bf16[512,4,128]{0,2,1:T(8,128)(2,1)} %bitcast.129, bf16[4,512,512]{2,1,0:T(8,128)(2,1)} %copy-done.1), kind=kOutput, calls=%fused_computation.86 | convolution fusion | flops 268435456 | bytes 3670016 | tf_op jit(solution)/shard_map/mhts,mthd->mshd/dot_general | solution.py:140
  157.1 2.2 %fusion.11 = bf16[4,128,512]{2,1,0:T(8,128)(2,1)} fusion(f32[4,128,512]{2,1,0:T(8,128)S(1)} %fusion.55, f32[512,4]{0,1:T(4,128)S(1)} %copy.96, bf16[512,4,128]{2,1,0:T(4,128)(2,1)S(1)} %copy-done.5, f32[1,4,128,128]{3,1,2,0:T(4,128)S(1)} %bitcast.125), kind=kOutput, calls=%fused_computation.20 | convolution fusion | flops 403701760 | bytes 2367488 | tf_op jit(solution)/shard_map/mshd,mhde->mshe/dot_general | solution.py:142
  159.3 2.0 %copy.115 = bf16[1,512,512]{2,1,0:T(8,128)(2,1)} copy(bf16[1,512,512]{1,2,0:T(8,128)(2,1)} %bitcast.130) | data formatting | bytes 1048576
  161.3 1.7 %convert_element_type.152 = f32[192,512]{1,0:T(8,128)} convert(bf16[192,512]{1,0:T(8,128)(2,1)} %reduce-scatter.5.cloned.1.call-done) | non-fusion elementwise | flops 98304 | bytes 589824 | tf_op jit(solution)/shard_map/convert_element_type | solution.py:100
  (39 shorter events, 1.1 us)
Async XLA Ops:
  7.2 64.5 %copy-start = (bf16[512,3072]{1,0:T(8,128)(2,1)S(1)}, bf16[512,3072]{1,0:T(8,128)(2,1)}, u32[]{:S(2)}) copy-start(bf16[512,3072]{1,0:T(8,128)(2,1)} %param.10) | copy-start | bytes 9437188
  7.2 50.1 %all-gather.2.cloned.1.call-start = ((), (), s32[]{:S(2)}) async-start(), calls=%async_computation.2 | async-start | bytes 4718592 | tf_op jit(solution)/shard_map/all_gather | solution.py:82
  7.9 124.1 %reduce-scatter.3.cloned.1.call-start = ((), (), s32[]{:S(2)}) async-start(), calls=%async_computation.3 | async-start | bytes 3932160 | tf_op jit(solution)/shard_map/reduce_scatter | solution.py:97
  45.1 2.8 %copy-start.10 = (pred[512,512]{1,0:T(8,128)(4,1)}, pred[512,512]{1,0:T(8,128)(4,1)S(1)}, u32[]{:S(2)}) copy-start(pred[512,512]{1,0:T(8,128)(4,1)S(1)} %iota_compare_fusion) | copy-start | bytes 786436
  45.1 4.1 %copy-start.6 = (bf16[512,4,128]{2,1,0:T(4,128)(2,1)S(1)}, bf16[512,4,128]{2,1,0:T(4,128)(2,1)}, u32[]{:S(2)}) copy-start(bf16[512,4,128]{2,1,0:T(4,128)(2,1)} %reshape.419) | copy-start | bytes 1572868
  47.9 1.3 copy-start.1
  49.2 1.0 copy-start.8
  71.4 89.9 %reduce-scatter.5.cloned.1.call-start = ((), (), s32[]{:S(2)}) async-start(), calls=%async_computation.4 | async-start | bytes 983040 | tf_op jit(solution)/shard_map/reduce_scatter | solution.py:100
  78.2 4.4 %copy-start.4 = (bf16[512,4,128]{2,1,0:T(4,128)(2,1)S(1)}, bf16[512,4,128]{2,1,0:T(4,128)(2,1)}, u32[]{:S(2)}) copy-start(bf16[512,4,128]{2,1,0:T(4,128)(2,1)} %reshape.425) | copy-start | bytes 1572868
  81.2 1.4 copy-start.2
  82.6 1.0 copy-start.9
  132.0 17.1 %copy-start.3 = (bf16[4,512,512]{2,1,0:T(8,128)(2,1)S(1)}, bf16[4,512,512]{2,1,0:T(8,128)(2,1)}, u32[]{:S(2)}) copy-start(bf16[4,512,512]{2,1,0:T(8,128)(2,1)} %copy-done.2) | copy-start | bytes 6291460
  132.0 18.7 %copy-start.7 = (bf16[512,4,128]{2,1,0:T(4,128)(2,1)S(1)}, bf16[512,4,128]{2,1,0:T(4,128)(2,1)}, u32[]{:S(2)}) copy-start(bf16[512,4,128]{2,1,0:T(4,128)(2,1)} %reshape.419) | copy-start | bytes 1572868
  154.8 2.3 %copy-start.5 = (bf16[512,4,128]{2,1,0:T(4,128)(2,1)S(1)}, bf16[512,4,128]{2,1,0:T(4,128)(2,1)}, u32[]{:S(2)}) copy-start(bf16[512,4,128]{2,1,0:T(4,128)(2,1)} %reshape.425) | copy-start | bytes 1572868
Sparse Core Ops, SparseCore 0:
  9.5 47.6 all-gather.1
  71.6 60.3 reduce-scatter.2
  134.5 23.1 reduce-scatter.4
where the time goes:
time: 171 us; the launch traced here: 170 us
  waiting for transfers between devices  47.1 us (28%)
  matrix products  37.6 us (22%)
  blocking collectives  33 us (19%)
  local copies, waits for them, and re-layouts  31.6 us (18%)
  between operations  14 us (8%)
  other arithmetic  6 us (4%)
    reduce_scatter x1, waiting for transfers between devices, local(): lax.psum_scatter(reordered.astype(jnp.bfloat16), 'seq', scatter_dimension...  41.6 us
    all_gather x1, blocking collectives, local(): lax.all_gather(local_state.reshape(1, micro_count, head_count, flat_size)...  17.4 us
    all_gather x1, blocking collectives, local(): lax.all_gather(local_back.reshape(1, micro_count, head_count, flat_size)....  15.6 us
    unnamed x25, local copies, waits for them, and re-layouts  9.27 us
    another operation x9, local copies, waits for them, and re-layouts  9.03 us
    dot_general x1, matrix products, local(): jnp.einsum('mcd,mcf->df', shard_piece, attn_out, preferred_element_type=j...  5.58 us
    all_gather x1, waiting for transfers between devices, local(): shard_piece = lax.all_gather(grad_out, 'tensor', axis=2, tiled=True)  4.74 us
    optimization_barrier x1, local copies, waits for them, and re-layouts, local(): lax.optimization_barrier((column_block * grad_scale).astype(jnp.bfloat16))  4.74 us
  transfers between devices with their start and end apart: 3, of which 2 were waited for; matrix products, arithmetic and copies ran while one was open for 33% of the time, Pallas kernels for 0%

commit v1 on v0

--- a/solution.py
+++ b/solution.py
@@ -6,6 +6,27 @@
 
 D = 3072
 highest_precision = lax.Precision.HIGHEST
+
+
+def in_order(pieces, dim):
+    pieces = jnp.moveaxis(pieces, 0, dim)
+    lengths = pieces.shape
+    return pieces.reshape(*lengths[:dim], lengths[dim] * lengths[dim + 1], *lengths[dim + 2 :])
+
+
+def doubled(x, axis):
+    peers, index = (lax.axis_size(axis), lax.axis_index(axis))
+    pieces, stride = (x[None], 1)
+    while stride < peers:
+        other = lax.ppermute(pieces, axis, [(i, i ^ stride) for i in range(peers)])
+        low = index & stride == 0
+        pieces = jnp.concatenate([jnp.where(low, pieces, other), jnp.where(low, other, pieces)])
+        stride *= 2
+    return pieces
+
+
+def doubled_up(x, axis, dim):
+    return in_order(doubled(x, axis), dim)
 
 
 def decay_matrix(cumulative):
@@ -110,11 +131,8 @@
         )
         * inverse
     )
-    shard_piece = lax.all_gather(
-        local_back.reshape(1, micro_count, head_count, flat_size).astype(jnp.bfloat16),
-        "seq",
-        axis=0,
-        tiled=True,
+    shard_piece = doubled_up(
+        local_back.reshape(1, micro_count, head_count, flat_size).astype(jnp.bfloat16), "seq", 0
     ).astype(jnp.float32)
     piece_rows = shard_piece.shape[0]
     position = jnp.arange(piece_rows, dtype=jnp.int32)

time: 171 us -> 196 us (1.15)
  waiting for transfers between devices: 47.1 us -> 74.9 us
  blocking collectives: 33 us -> 17.4 us
  matrix products: 37.6 us -> 41.9 us
  other arithmetic: 6 us -> 10.2 us
  starting transfers between devices: 0.3 us -> 4.36 us
    ppermute x0 -> x2, waiting for transfers between devices: none -> 26.2 us  [doubled(): other = lax.ppermute(pieces, axis, [(i, i ^ stride) for i in range(peers)])]
    all_gather x1 -> x0, blocking collectives: 15.6 us -> none  [local(): lax.all_gather(local_back.reshape(1, micro_count, head_count, flat_size)....]
    reduce_scatter x1, waiting for transfers between devices: 0.01 us -> 14.2 us  [local(): lax.psum_scatter(reduced, 'dp', scatter_dimension=0, tiled=True)]
    reduce_scatter x1, waiting for transfers between devices: 41.6 us -> 29.6 us  [local(): lax.psum_scatter(reordered.astype(jnp.bfloat16), 'seq', scatter_dimension...]
    ppermute x0 -> x2, starting transfers between devices: none -> 4.02 us  [doubled(): other = lax.ppermute(pieces, axis, [(i, i ^ stride) for i in range(peers)])]
    dot_general x1, matrix products: 0.81 us -> 3.66 us  [local(): jnp.einsum('mhts,mshd->mthd', grad_weights, key_heads, preferred_element_...]
    select_n x0 -> x2, other arithmetic: none -> 2.03 us  [doubled(): jnp.where(low, pieces, other)]
    unnamed x25 -> x35, local copies, waits for them, and re-layouts: 9.27 us -> 8.59 us
  transfers between devices with their start and end apart: 3 -> 5, of which waited for: 2 -> 4; matrix products, arithmetic and copies ran while one was open for 33% -> 32% of each run, Pallas kernels for 0% -> 0%
where the time goes in v1:
time: 196 us; the launch traced here: 195 us
  waiting for transfers between devices  74.9 us (38%)
  matrix products  41.9 us (21%)
  local copies, waits for them, and re-layouts  31.7 us (16%)
  blocking collectives  17.4 us (9%)
  between operations  14 us (7%)
  other arithmetic  10.2 us (5%)
  starting transfers between devices  4.36 us (2%)
    reduce_scatter x1, waiting for transfers between devices, local(): lax.psum_scatter(reordered.astype(jnp.bfloat16), 'seq', scatter_dimension...  29.6 us
    ppermute x2, waiting for transfers between devices, doubled(): other = lax.ppermute(pieces, axis, [(i, i ^ stride) for i in range(peers)])  26.2 us
    all_gather x1, blocking collectives, local(): lax.all_gather(local_state.reshape(1, micro_count, head_count, flat_size)...  17.4 us
    reduce_scatter x1, waiting for transfers between devices, local(): lax.psum_scatter(reduced, 'dp', scatter_dimension=0, tiled=True)  14.2 us
    another operation x9, local copies, waits for them, and re-layouts  9.03 us
    unnamed x35, local copies, waits for them, and re-layouts  8.59 us
    dot_general x1, matrix products, local(): jnp.einsum('mcd,mcf->df', shard_piece, attn_out, preferred_element_type=j...  5.69 us
    optimization_barrier x1, local copies, waits for them, and re-layouts, local(): lax.optimization_barrier((column_block * grad_scale).astype(jnp.bfloat16))  4.66 us
  transfers between devices with their start and end apart: 5, of which 4 were waited for; matrix products, arithmetic and copies ran while one was open for 32% of the time, Pallas kernels for 0%

profile of v1, /device:TPU:0, one launch (start us, length us, event | category | flops | bytes accessed | tf_op | source)
XLA Modules:
  0.0 194.5 jit_solution(16194467669418107654)
XLA Ops:
  7.2 0.7 all-gather.2.cloned.1.call-update
  8.0 0.8 constant_dynamic-slice_fusion
  8.8 1.2 reduce-window.6
  10.4 0.9 copy.129
  11.2 0.8 reshape.432
  12.3 2.0 %reshape.422 = bf16[512,4,128]{2,1,0:T(4,128)(2,1)} reshape(bf16[1,512,512]{2,1,0:T(8,128)(2,1)} %param.8) | data formatting | bytes 1048576 | tf_op jit(solution)/shard_map/reshape.6
  14.2 2.0 %reshape.428 = bf16[512,4,128]{2,1,0:T(4,128)(2,1)} reshape(bf16[1,512,512]{2,1,0:T(8,128)(2,1)} %param.7) | data formatting | bytes 1048576 | tf_op jit(solution)/shard_map/reshape.13
  16.2 1.7 exponential_bitcast_fusion
  17.9 1.1 copy.100
  19.3 0.8 exponential_bitcast_fusion.1
  20.0 1.1 copy.96
  21.1 2.6 %convolution_convert_fusion = bf16[4,128,128]{2,1,0:T(8,128)(2,1)S(1)} fusion(f32[512,4]{0,1:T(4,128)S(1)} %copy.96, bf16[512,4,128]{2,1,0:T(4,128)(2,1)} %reshape.428, bf16[512,4,128]{2,1,0:T(4,128)(2,1)} %reshape.422), kind=kOutput, calls=%fused_computation.24 | convolution fusion | flops 403243008 | bytes 1187840 | tf_op jit(solution)/shard_map/mshd,mshe->mhde/dot_general | solution.py:72
  24.0 17.4 %all_gather.7 = bf16[4,1,4,16384]{3,2,1,0:T(4,128)(2,1)S(1)} all-gather(bf16[1,1,4,16384]{3,2,1,0:T(4,128)(2,1)S(1)} %convert_element_type.129), channel_id=1, replica_groups=mesh['dp'=4,'seq'=4,'tensor'=2] {'seq'}, dimensions={0}, use_global_device_ids=true | all-gather | bytes 655360 | tf_op jit(solution)/shard_map/all_gather | solution.py:75
  42.1 1.3 fusion.26
  43.6 2.0 %reshape.435 = bf16[512,4,128]{2,1,0:T(4,128)(2,1)} reshape(bf16[1,512,512]{2,1,0:T(8,128)(2,1)} %param.6) | data formatting | bytes 1048576 | tf_op jit(solution)/shard_map/reshape.52
  45.7 2.8 %multiply_convert_fusion.1 = bf16[4,512,512]{2,1,0:T(8,128)(2,1)S(1)} fusion(f32[4,512]{1,0:T(4,128)S(1)} %bitcast_add_fusion.1, pred[512,512]{1,0:T(8,128)(4,1)S(1)} %iota_compare_fusion, bf16[512,4,128]{2,1,0:T(4,128)(2,1)} %reshape.435, bf16[512,4,128]{2,1,0:T(4,128)(2,1)} %reshape.428), kind=kOutput, calls=%fused_computation.1 | convolution fusion | flops 274726912 | bytes 3416064 | tf_op jit(solution)/shard_map/mthd,mshd->mhts/dot_general | solution.py:68
  48.5 1.4 copy-done.1
  49.9 0.8 convolution_bitcast_fusion.1
  50.9 2.2 %fusion.12 = bf16[4,128,512]{2,1,0:T(8,128)(2,1)} fusion(f32[4,128,512]{2,1,0:T(8,128)S(1)} %convolution_bitcast_fusion.1, f32[512,4]{0,1:T(4,128)S(1)} %copy.100, bf16[512,4,128]{2,1,0:T(4,128)(2,1)S(1)} %copy-done.6, f32[1,4,128,128]{3,1,2,0:T(4,128)S(1)} %bitcast.123), kind=kOutput, calls=%fused_computation.21 | convolution fusion | flops 403963904 | bytes 2367488 | tf_op jit(solution)/shard_map/mthd,mhde->mthe/dot_general | solution.py:95
  53.1 4.1 %all-gather.2.cloned.1.call-done = bf16[1,512,3072]{2,1,0:T(8,128)(2,1)} async-done(((bf16[1,512,1536]{2,1,0:T(8,128)(2,1)}), bf16[1,512,3072]{2,1,0:T(8,128)(2,1)}) %all-gather.2.cloned.1.call-update) | async-done | bytes 3145744 | tf_op jit(solution)/shard_map/all_gather | solution.py:103
  57.2 3.8 %fusion.6 = bf16[512,512]{0,1:T(8,128)(2,1)S(1)} fusion(bf16[512,3072]{1,0:T(8,128)(2,1)S(1)} %copy-done, bf16[1,512,3072]{2,1,0:T(8,128)(2,1)} %all-gather.2.cloned.1.call-done), kind=kOutput, calls=%fused_computation.17 | convolution fusion | flops 1610874880 | bytes 6815744 | tf_op jit(solution)/shard_map/mcd,fd->mcf/dot_general | solution.py:104
  61.0 0.8 copy-done.10
  61.8 2.8 %multiply_convert_fusion.2 = bf16[4,512,512]{2,1,0:T(8,128)(2,1)} fusion(bf16[512,4,128]{0,2,1:T(8,128)(2,1)S(1)} %bitcast.127, f32[4,512]{1,0:T(4,128)S(1)} %bitcast_add_fusion.1, pred[512,512]{1,0:T(8,128)(4,1)S(1)} %copy-done.14, bf16[512,4,128]{2,1,0:T(4,128)(2,1)S(1)} %copy-done.4), kind=kOutput, calls=%fused_computation.2 | convolution fusion | flops 274726912 | bytes 3416064 | tf_op jit(solution)/shard_map/mthd,mshd->mhts/dot_general | solution.py:124
  64.7 2.0 %copy.99 = bf16[512,4,128]{2,0,1:T(8,128)(2,1)} copy(bf16[512,4,128]{0,2,1:T(8,128)(2,1)} %bitcast.128) | data formatting | bytes 1048576 | tf_op jit(solution)/shard_map/reshape.5
  66.7 3.7 %convolution_bitcast_fusion.2 = f32[4,128,512]{2,1,0:T(8,128)} fusion(bf16[4,512,512]{2,1,0:T(8,128)(2,1)} %multiply_convert_fusion.2, bf16[512,4,128]{2,1,0:T(4,128)(2,1)} %reshape.428), kind=kOutput, calls=%fused_computation.10 | convolution fusion | flops 268435456 | bytes 3670016 | tf_op jit(solution)/shard_map/mhts,mshd->mthd/dot_general | solution.py:149
  70.4 1.5 convolution_bitcast_fusion
  71.9 2.0 %fusion.13 = bf16[4,128,128]{2,1,0:T(8,128)(2,1)} fusion(bf16[512,4,128]{0,2,1:T(8,128)(2,1)S(1)} %bitcast.130, f32[512,4]{0,1:T(4,128)S(1)} %copy.100, bf16[512,4,128]{2,1,0:T(4,128)(2,1)S(1)} %copy-done.7), kind=kOutput, calls=%fused_computation.23 | convolution fusion | flops 403308544 | bytes 1187840 | tf_op jit(solution)/shard_map/mthd,mthe->mhde/dot_general | solution.py:129
  73.9 0.9 convert_element_type.136
  74.8 1.6 collective-permute-start
  76.4 5.7 %fusion = bf16[3072,512]{0,1:T(8,128)(2,1)} fusion(bf16[512,512]{0,1:T(8,128)(2,1)} %bitcast.136, bf16[1,512,3072]{2,1,0:T(8,128)(2,1)} %all-gather.2.cloned.1.call-done), kind=kOutput, calls=%fused_computation.4 | convolution fusion | flops 1613758464 | bytes 6815744 | tf_op jit(solution)/shard_map/mcd,mcf->df/dot_general | solution.py:105
  82.1 2.1 %fusion.9 = bf16[4,128,512]{2,1,0:T(8,128)(2,1)} fusion(f32[4,128,512]{2,1,0:T(8,128)S(1)} %copy-done.9, bf16[512,4,128]{2,0,1:T(8,128)(2,1)S(1)} %copy-done.12, f32[512,4]{0,1:T(4,128)S(1)} %copy.100, f32[1,4,128,128]{3,1,2,0:T(4,128)S(1)} %bitcast.124), kind=kOutput, calls=%fused_computation.18 | convolution fusion | flops 403963904 | bytes 2367488 | tf_op jit(solution)/shard_map/mthe,mhde->mthd/dot_general | solution.py:150
  84.2 2.0 %copy.113 = bf16[1,512,512]{2,1,0:T(8,128)(2,1)} copy(bf16[1,512,512]{1,2,0:T(8,128)(2,1)} %bitcast.131) | data formatting | bytes 1048576
  86.2 4.7 %copy.111 = bf16[3072,512]{1,0:T(8,128)(2,1)} copy(bf16[3072,512]{0,1:T(8,128)(2,1)} %fusion) | data formatting | bytes 6291456 | tf_op jit(solution)/shard_map/optimization_barrier | solution.py:109
  90.9 3.9 %copy.112 = bf16[4,4,192,512]{3,2,1,0:T(8,128)(2,1)} copy(bf16[4,4,192,512]{3,2,0,1:T(8,128)(2,1)} %bitcast.122) | data formatting | bytes 6291456 | tf_op jit(solution)/shard_map/convert_element_type | solution.py:119
  95.1 1.0 broadcast_select_fusion.3
  96.3 2.5 %collective-permute-start.1 = (bf16[2,1,1,4,16384]{4,3,2,1,0:T(4,128)(2,1)S(1)}, bf16[2,1,1,4,16384]{4,3,2,1,0:T(4,128)(2,1)S(1)}, u32[]{:S(2)}, u32[]{:S(2)}) collective-permute-start(bf16[2,1,1,4,16384]{4,3,2,1,0:T(4,128)(2,1)S(1)} %pad_maximum_fusion), channel_id=1, source_target_pairs={{0,4},{2,6},{4,0},{6,2},{1,5},{3,7},{5,1},{7,3},{8,12},{10,14},{12... | collective-permute-start | bytes 786440 | tf_op jit(solution)/shard_map/ppermute | solution.py:21
  98.8 3.7 %fusion.55 = f32[4,128,512]{2,1,0:T(8,128)} fusion(bf16[512,4,128]{0,2,1:T(8,128)(2,1)} %bitcast.129, bf16[4,512,512]{2,1,0:T(8,128)(2,1)} %copy-done.1), kind=kOutput, calls=%fused_computation.92 | convolution fusion | flops 268435456 | bytes 3670016 | tf_op jit(solution)/shard_map/mhts,mthd->mshd/dot_general | solution.py:158
  102.5 26.2 %collective-permute-done.1 = bf16[2,1,1,4,16384]{4,3,2,1,0:T(4,128)(2,1)S(1)} collective-permute-done((bf16[2,1,1,4,16384]{4,3,2,1,0:T(4,128)(2,1)S(1)}, bf16[2,1,1,4,16384]{4,3,2,1,0:T(4,128)(2,1)S(1)}, u32[]{:S(2)}, u32[]{:S(2)}) %collective-permute-start.1) | collective-permute-done | bytes 262176 | tf_op jit(solution)/shard_map/ppermute | solution.py:21
  128.7 1.0 broadcast_select_fusion.1
  129.7 29.6 %reduce-scatter.3.cloned.1.call-done = bf16[768,512]{1,0:T(8,128)(2,1)} async-done(((bf16[3072,512]{1,0:T(8,128)(2,1)}), bf16[768,512]{1,0:T(8,128)(2,1)}) %reduce-scatter.3.cloned.1.call-update) | async-done | bytes 786448 | tf_op jit(solution)/shard_map/reduce_scatter | solution.py:118
  159.4 1.4 maximum_bitcast_fusion
  160.8 1.3 fusion.24
  162.4 2.1 %fusion.10 = bf16[4,128,512]{2,1,0:T(8,128)(2,1)} fusion(f32[4,128,512]{2,1,0:T(8,128)S(1)} %copy-done.8, f32[512,4]{0,1:T(4,128)S(1)} %copy.96, bf16[512,4,128]{2,1,0:T(4,128)(2,1)S(1)} %copy-done.5, f32[1,4,128,128]{3,1,2,0:T(4,128)S(1)} %bitcast.125), kind=kOutput, calls=%fused_computation.19 | convolution fusion | flops 403701760 | bytes 2367488 | tf_op jit(solution)/shard_map/mshe,mhde->mshd/dot_general | solution.py:157
  164.4 2.0 %copy.114 = bf16[1,512,512]{2,1,0:T(8,128)(2,1)} copy(bf16[1,512,512]{1,2,0:T(8,128)(2,1)} %bitcast.133) | data formatting | bytes 1048576
  166.5 3.6 %fusion.11 = bf16[4,128,512]{2,1,0:T(8,128)(2,1)} fusion(f32[4,128,512]{2,1,0:T(8,128)} %fusion.55, f32[512,4]{0,1:T(4,128)S(1)} %copy.96, bf16[512,4,128]{2,1,0:T(4,128)(2,1)} %reshape.428, f32[1,4,128,128]{3,1,2,0:T(4,128)S(1)} %bitcast.126), kind=kOutput, calls=%fused_computation.20 | convolution fusion | flops 403701760 | bytes 2367488 | tf_op jit(solution)/shard_map/mshd,mhde->mshe/dot_general | solution.py:160
  170.0 2.1 %copy.115 = bf16[1,512,512]{2,1,0:T(8,128)(2,1)} copy(bf16[1,512,512]{1,2,0:T(8,128)(2,1)} %bitcast.132) | data formatting | bytes 1048576
  172.1 14.2 %reduce-scatter.5.cloned.1.call-done = bf16[192,512]{1,0:T(8,128)(2,1)} async-done(((bf16[768,512]{1,0:T(8,128)(2,1)}), bf16[192,512]{1,0:T(8,128)(2,1)}) %reduce-scatter.5.cloned.1.call-update) | async-done | bytes 196624 | tf_op jit(solution)/shard_map/reduce_scatter | solution.py:121
  186.3 1.7 convert_element_type.153
  (56 shorter events, 3.1 us)
Async XLA Ops:
  7.2 50.1 %copy-start = (bf16[512,3072]{1,0:T(8,128)(2,1)S(1)}, bf16[512,3072]{1,0:T(8,128)(2,1)}, u32[]{:S(2)}) copy-start(bf16[512,3072]{1,0:T(8,128)(2,1)} %param.10) | copy-start | bytes 9437188
  7.2 50.1 %all-gather.2.cloned.1.call-start = ((), (), s32[]{:S(2)}) async-start(), calls=%async_computation.2 | async-start | bytes 4718592 | tf_op jit(solution)/shard_map/all_gather | solution.py:103
  7.9 151.4 %reduce-scatter.3.cloned.1.call-start = ((), (), s32[]{:S(2)}) async-start(), calls=%async_computation.3 | async-start | bytes 3932160 | tf_op jit(solution)/shard_map/reduce_scatter | solution.py:118
  45.7 2.8 %copy-start.13 = (pred[512,512]{1,0:T(8,128)(4,1)}, pred[512,512]{1,0:T(8,128)(4,1)S(1)}, u32[]{:S(2)}) copy-start(pred[512,512]{1,0:T(8,128)(4,1)S(1)} %iota_compare_fusion) | copy-start | bytes 786436
  45.7 4.2 %copy-start.3 = (bf16[512,4,128]{2,1,0:T(4,128)(2,1)S(1)}, bf16[512,4,128]{2,1,0:T(4,128)(2,1)}, u32[]{:S(2)}) copy-start(bf16[512,4,128]{2,1,0:T(4,128)(2,1)} %reshape.422) | copy-start | bytes 1572868
  48.5 1.4 copy-start.1
  49.9 1.0 copy-start.6
  57.2 4.6 %copy-start.4 = (bf16[512,4,128]{2,1,0:T(4,128)(2,1)S(1)}, bf16[512,4,128]{2,1,0:T(4,128)(2,1)}, u32[]{:S(2)}) copy-start(bf16[512,4,128]{2,1,0:T(4,128)(2,1)} %reshape.422) | copy-start | bytes 1572868
  57.2 4.6 %copy-start.14 = (pred[512,512]{1,0:T(8,128)(4,1)S(1)}, pred[512,512]{1,0:T(8,128)(4,1)}, u32[]{:S(2)}) copy-start(pred[512,512]{1,0:T(8,128)(4,1)} %copy-done.13) | copy-start | bytes 786436
  61.0 0.8 copy-start.10
  66.7 3.7 %copy-start.2 = (bf16[4,512,512]{2,1,0:T(8,128)(2,1)S(1)}, bf16[4,512,512]{2,1,0:T(8,128)(2,1)}, u32[]{:S(2)}) copy-start(bf16[4,512,512]{2,1,0:T(8,128)(2,1)} %multiply_convert_fusion.2) | copy-start | bytes 6291460
  66.7 3.7 %copy-start.7 = (bf16[512,4,128]{2,1,0:T(4,128)(2,1)S(1)}, bf16[512,4,128]{2,1,0:T(4,128)(2,1)}, u32[]{:S(2)}) copy-start(bf16[512,4,128]{2,1,0:T(4,128)(2,1)} %reshape.435) | copy-start | bytes 1572868
  66.7 5.1 %copy-start.11 = (bf16[512,512]{0,1:T(8,128)(2,1)S(1)}, bf16[512,512]{0,1:T(8,128)(2,1)}, u32[]{:S(2)}) copy-start(bf16[512,512]{0,1:T(8,128)(2,1)} %copy-done.10) | copy-start | bytes 1572868
  74.8 20.2 %collective-permute-start = (bf16[1,1,1,4,16384]{4,3,2,1,0:T(4,128)(2,1)S(1)}, bf16[1,1,1,4,16384]{4,3,2,1,0:T(4,128)(2,1)}, u32[]{:S(2)}, u32[]{:S(2)}) collective-permute-start(bf16[1,1,1,4,16384]{4,3,2,1,0:T(4,128)(2,1)S(1)} %convert_element_type.136), channel_id=1, source_target_pairs={{0,2},{2,0},{4,6},{6,4},{1,3},{3,1},{5,7},{7,5},{8,10},{10,8},{12,... | collective-permute-start | bytes 393224 | tf_op jit(solution)/shard_map/ppermute | solution.py:21
  76.4 5.7 %copy-start.9 = (f32[4,128,512]{2,1,0:T(8,128)S(1)}, f32[4,128,512]{2,1,0:T(8,128)}, u32[]{:S(2)}) copy-start(f32[4,128,512]{2,1,0:T(8,128)} %convolution_bitcast_fusion.2) | copy-start | bytes 3145732
  76.4 5.7 %copy-start.12 = (bf16[512,4,128]{2,0,1:T(8,128)(2,1)S(1)}, bf16[512,4,128]{2,0,1:T(8,128)(2,1)}, u32[]{:S(2)}) copy-start(bf16[512,4,128]{2,0,1:T(8,128)(2,1)} %copy.99) | copy-start | bytes 1572868
  94.8 91.5 %reduce-scatter.5.cloned.1.call-start = ((), (), s32[]{:S(2)}) async-start(), calls=%async_computation.4 | async-start | bytes 983040 | tf_op jit(solution)/shard_map/reduce_scatter | solution.py:121
  96.3 64.5 %copy-start.15 = (f32[4,4]{1,0:T(4,128)S(1)}, f32[4,4]{1,0:T(4,128)}, u32[]{:S(2)}) copy-start(f32[4,4]{1,0:T(4,128)} %get-tuple-element.26) | copy-start | bytes 196
  96.3 32.4 %collective-permute-start.1 = (bf16[2,1,1,4,16384]{4,3,2,1,0:T(4,128)(2,1)S(1)}, bf16[2,1,1,4,16384]{4,3,2,1,0:T(4,128)(2,1)S(1)}, u32[]{:S(2)}, u32[]{:S(2)}) collective-permute-start(bf16[2,1,1,4,16384]{4,3,2,1,0:T(4,128)(2,1)S(1)} %pad_maximum_fusion), channel_id=1, source_target_pairs={{0,4},{2,6},{4,0},{6,2},{1,5},{3,7},{5,1},{7,3},{8,12},{10,14},{12... | collective-permute-start | bytes 786440 | tf_op jit(solution)/shard_map/ppermute | solution.py:21
  159.4 3.0 %copy-start.5 = (bf16[512,4,128]{2,1,0:T(4,128)(2,1)S(1)}, bf16[512,4,128]{2,1,0:T(4,128)(2,1)}, u32[]{:S(2)}) copy-start(bf16[512,4,128]{2,1,0:T(4,128)(2,1)} %reshape.422) | copy-start | bytes 1572868
  159.4 3.0 %copy-start.8 = (f32[4,128,512]{2,1,0:T(8,128)S(1)}, f32[4,128,512]{2,1,0:T(8,128)}, u32[]{:S(2)}) copy-start(f32[4,128,512]{2,1,0:T(8,128)} %convolution_bitcast_fusion) | copy-start | bytes 3145732
Sparse Core Ops, SparseCore 0:
  9.5 47.6 all-gather.1
  94.9 64.3 reduce-scatter.2
  161.9 24.3 reduce-scatter.4
